TPU v7x, 32 devices: a whole 2x2x4 slice. The times are simulated.
32 devices in a mesh: leaf: 8 (over z, y), row: 4 (over x, core).
Axes of the slice: x: 2, y: 2, z: 4, core: 2. Of those that a mesh axis runs over, the one named last changes fastest.
Arguments:
- rhs_blocks: float32 [7, 1024, 256], P(None, 'leaf'), may hold values from -6 to 6
- diag_inverse: float32 [7, 1024, 1024], P(None, 'leaf', 'row'), may hold values from -0.1875 to 0.1875
- lower_blocks: float32 [6, 1024, 1024], P(None, 'leaf', 'row'), may hold values from -0.09375 to 0.09375
- update_rows: int32 [6, 1024], P(None, 'leaf'), may hold values from 512 to 895, as said below
Outputs:
- solution: float32 [7, 1024, 256], P(None, 'leaf')
Inputs may be any that keep to these rules, and one draw needn't show every extreme that they name: update_rows[s, m] = a * 128 + c names column i * 128 + c of an ancestor a of supernode s, where i = m // 128; the 128 entries of one supernode with the same i are distinct.
All inputs are finite; a program needn't handle non-finite values.
Results may differ from a plain program's by a relative error of at most 0.0001.
Values sent between devices are 32-bit elements; how exact they have to be, the bound alone decides.
No kernel may reach another device: no remote copies, remote signals or barrier semaphores. Data moves between devices by JAX's collectives and lax.ppermute only.
A program may use at most 64 MiB of HBM per device.

v0:
```python
import jax
import jax.numpy as jnp
from jax import lax
from jax.sharding import PartitionSpec as P


def local(rhs_blocks, diag_inverse, lower_blocks, update_rows):
    leaf_count = lax.axis_size("leaf")
    node_total = rhs_blocks.shape[0]
    panel_rows = rhs_blocks.shape[1]
    rhs_width = rhs_blocks.shape[2]
    level_total = (node_total + 1).bit_length() - 1
    slice_rows = diag_inverse.shape[2] // leaf_count
    current = rhs_blocks.reshape(node_total * panel_rows, rhs_width)
    stored_slices = [None] * level_total
    for depth_level in range(level_total - 1, -1, -1):
        first_node = 2**level_total - 2 ** (depth_level + 1)
        node_count = 2**depth_level
        stop_node = first_node + node_count
        diag_part = diag_inverse[first_node:stop_node]
        lower_part = lower_blocks[first_node:stop_node] if depth_level > 0 else None
        local_rhs = current[first_node * panel_rows : stop_node * panel_rows].reshape(
            node_count, panel_rows, rhs_width
        )
        partial_value = jnp.einsum(
            "scr,sct->rst", diag_part, local_rhs, precision=lax.Precision.HIGHEST
        )
        complete = lax.psum(partial_value, "leaf")
        stored = lax.dynamic_slice_in_dim(
            complete, lax.axis_index("leaf") * slice_rows, slice_rows, 0
        )
        if depth_level > 0:
            update = jnp.einsum(
                "smr,rst->smt", lower_part, complete, precision=lax.Precision.HIGHEST
            )
        stored_slices[depth_level] = stored
        if depth_level > 0:
            update = lax.psum(update, "row")
            targets = update_rows[first_node:stop_node].reshape(-1)
            current = current.at[targets].add(-update.reshape(-1, rhs_width))
    answer = jnp.zeros((node_total * panel_rows, rhs_width), jnp.float32)
    for depth_level in range(level_total):
        first_node = 2**level_total - 2 ** (depth_level + 1)
        node_count = 2**depth_level
        stop_node = first_node + node_count
        diag_part = diag_inverse[first_node:stop_node]
        residual = stored_slices[depth_level]
        if depth_level > 0:
            lower_part = lower_blocks[first_node:stop_node]
            targets = update_rows[first_node:stop_node].reshape(-1)
            known = answer[targets].reshape(node_count, panel_rows, rhs_width)
            residual = residual - lax.psum_scatter(
                jnp.einsum("smr,smt->rst", lower_part, known, precision=lax.Precision.HIGHEST),
                "leaf",
                scatter_dimension=0,
                tiled=True,
            )
        partial_value = jnp.einsum(
            "scr,rst->sct",
            diag_part,
            lax.all_gather(residual, "leaf", axis=0, tiled=True),
            precision=lax.Precision.HIGHEST,
        )
        solved = lax.psum(partial_value, "row")
        answer = answer.at[first_node * panel_rows : stop_node * panel_rows].set(
            solved.reshape(-1, rhs_width)
        )
    return answer.reshape(node_total, panel_rows, rhs_width)


def solution(mesh):
    placed = (
        P(None, "leaf", None),
        P(None, "leaf", "row"),
        P(None, "leaf", "row"),
        P(None, "leaf"),
    )
    return jax.shard_map(
        local, mesh=mesh, in_specs=placed, out_specs=P(None, "leaf", None), check_vma=False
    )
```

profile of v0, /device:TPU:0, one launch (start us, length us, event | category | flops | bytes accessed | tf_op | source)
XLA Modules:
  0.0 698.2 jit_solution(705623157416841822)
XLA Ops:
  6.5 1.3 copy.104
  7.8 0.2 copy-done
  8.0 2.0 convolution_bitcast_fusion.1
  10.1 81.5 %all-reduce.14.cloned.1.call-done = f32[256,4,256]{2,0,1:T(8,128)} async-done(((f32[256,4,256]{2,0,1:T(8,128)}), f32[256,4,256]{2,0,1:T(8,128)}) %all-reduce.14.cloned.1.call-update) | async-done | bytes 1048592 | tf_op jit(solution)/shard_map/psum | solution.py:28
  91.6 3.9 convolution_bitcast_fusion.4
  95.5 0.0 all-reduce.18.cloned.1.call-start
  95.6 0.6 slice-done
  96.2 32.2 %all-reduce.16.cloned.1.call-done = f32[4,128,256]{1,2,0:T(8,128)} async-done(((f32[4,128,256]{1,2,0:T(8,128)}), f32[4,128,256]{1,2,0:T(8,128)}) %all-reduce.16.cloned.1.call-update) | async-done | bytes 524304 | tf_op jit(solution)/shard_map/psum | solution.py:38
  128.4 1.9 neg.12
  130.3 1.2 copy.47
  131.6 3.7 scatter_fusion
  135.3 1.4 convolution_bitcast_fusion.3
  136.7 0.0 all-reduce.20.cloned.1.call-start
  136.8 0.6 copy-done.3
  137.4 71.9 %all-reduce.18.cloned.1.call-done = f32[256,2,256]{2,0,1:T(8,128)} async-done(((f32[256,2,256]{2,0,1:T(8,128)}), f32[256,2,256]{2,0,1:T(8,128)}) %all-reduce.18.cloned.1.call-update) | async-done | bytes 524304 | tf_op jit(solution)/shard_map/psum | solution.py:28
  209.3 2.8 convolution_bitcast_fusion.5
  212.1 0.0 all-reduce.22.cloned.1.call-start
  212.1 31.3 %all-reduce.20.cloned.1.call-done = f32[2,128,256]{1,2,0:T(8,128)} async-done(((f32[2,128,256]{1,2,0:T(8,128)}), f32[2,128,256]{1,2,0:T(8,128)}) %all-reduce.20.cloned.1.call-update) | async-done | bytes 262160 | tf_op jit(solution)/shard_map/psum | solution.py:38
  243.5 1.0 neg.14
  244.5 0.1 copy.51
  244.6 2.3 scatter_fusion.1
  246.9 1.1 convolution_bitcast_fusion.6
  248.0 0.0 all-reduce.24.cloned.1.call-start
  248.1 70.6 %all-reduce.22.cloned.1.call-done = f32[256,1,256]{0,2,1:T(8,128)} async-done(((f32[256,1,256]{0,2,1:T(8,128)}), f32[256,1,256]{0,2,1:T(8,128)}) %all-reduce.22.cloned.1.call-update) | async-done | bytes 262160 | tf_op jit(solution)/shard_map/psum | solution.py:28
  318.8 1.0 constant_dynamic-slice_fusion
  319.8 0.1 copy.52
  319.8 30.8 %all_gather.9 = f32[256,1,256]{2,1,0:T(1,128)S(1)} all-gather(f32[32,1,256]{2,1,0:T(1,128)S(1)} %copy.52), channel_id=1, replica_groups=mesh['leaf'=8,'row'=4] {'leaf'}, dimensions={0}, use_global_device_ids=true | all-gather | bytes 294912 | tf_op jit(solution)/shard_map/all_gather | solution.py:61
  350.6 1.3 convolution_bitcast_fusion.7
  351.9 0.0 all-reduce.30.cloned.1.call-start
  352.0 30.8 %all-reduce.24.cloned.1.call-done = f32[128,256]{0,1:T(8,128)} async-done(((f32[128,256]{0,1:T(8,128)}), f32[128,256]{0,1:T(8,128)}) %all-reduce.24.cloned.1.call-update) | async-done | bytes 131088 | tf_op jit(solution)/shard_map/psum | solution.py:64
  382.8 1.0 scatter.10
  383.7 0.3 copy.53
  384.1 1.7 gather_fusion
  385.7 1.6 convolution_bitcast_fusion.2
  387.3 1.0 copy.55
  388.3 0.0 all-reduce.26.cloned.1.call-start
  388.4 0.6 copy-done.4
  389.0 0.6 dynamic-slice.20
  390.3 70.6 %all-reduce.30.cloned.1.call-done = f32[256,2,256]{2,1,0:T(2,128)} async-done(((f32[256,2,256]{2,1,0:T(2,128)}), f32[256,2,256]{2,1,0:T(2,128)}) %all-reduce.30.cloned.1.call-update) | async-done | bytes 524304
  460.9 0.8 constant_dynamic-slice_fusion.2
  461.7 0.8 copy_subtract_fusion.1
  462.6 0.1 copy.57
  462.6 31.8 %all_gather.10 = f32[256,2,256]{2,1,0:T(2,128)S(1)} all-gather(f32[32,2,256]{2,1,0:T(2,128)S(1)} %copy.57), channel_id=1, replica_groups=mesh['leaf'=8,'row'=4] {'leaf'}, dimensions={0}, use_global_device_ids=true | all-gather | bytes 589824 | tf_op jit(solution)/shard_map/all_gather | solution.py:61
  494.4 0.5 fusion.2
  494.8 0.8 copy.75
  495.7 0.0 all-reduce.32.cloned.1.call-start
  495.8 31.2 %all-reduce.26.cloned.1.call-done = f32[256,256]{0,1:T(8,128)} async-done(((f32[256,256]{0,1:T(8,128)}), f32[256,256]{0,1:T(8,128)}) %all-reduce.26.cloned.1.call-update) | async-done | bytes 262160 | tf_op jit(solution)/shard_map/psum | solution.py:64
  527.0 1.0 constant_dynamic-update-slice_fusion.1
  528.0 0.3 copy.60
  528.3 1.6 gather_fusion.1
  529.8 2.1 convolution_bitcast_fusion
  531.9 1.3 copy.62
  533.3 0.0 all-gather.2.cloned.1.call-start
  533.3 78.3 %all-reduce.32.cloned.1.call-done = f32[256,4,256]{2,1,0:T(4,128)} async-done(((f32[256,4,256]{2,1,0:T(4,128)}), f32[256,4,256]{2,1,0:T(4,128)}) %all-reduce.32.cloned.1.call-update) | async-done | bytes 1048592
  611.6 0.9 constant_dynamic-slice_fusion.1
  612.5 0.9 copy_subtract_fusion
  613.5 0.7 copy.64
  614.2 0.0 all-reduce.28.cloned.1.call-start
  614.3 39.8 %all-gather.2.cloned.1.call-done = f32[256,4,256]{2,1,0:T(4,128)} async-done(((f32[32,4,256]{2,1,0:T(4,128)}), f32[256,4,256]{2,1,0:T(4,128)}) %all-gather.2.cloned.1.call-update) | async-done | bytes 1048592 | tf_op jit(solution)/shard_map/all_gather | solution.py:61
  654.1 2.1 fusion
  656.2 1.0 copy.76
  657.3 32.1 %all-reduce.28.cloned.1.call-done = f32[512,256]{0,1:T(8,128)} async-done(((f32[512,256]{0,1:T(8,128)}), f32[512,256]{0,1:T(8,128)}) %all-reduce.28.cloned.1.call-update) | async-done | bytes 524304 | tf_op jit(solution)/shard_map/psum | solution.py:64
  689.3 1.1 constant_dynamic-update-slice_fusion
  690.4 1.2 copy.67
  (27 shorter events, 0.3 us)
Async XLA Ops:
  6.5 1.5 copy-start
  6.5 85.1 %all-reduce.14.cloned.1.call-start = ((), (), s32[]{:S(2)}) async-start(), calls=%async_computation | async-start | bytes 2097152 | tf_op jit(solution)/shard_map/psum | solution.py:28
  10.0 81.6 %copy-start.2 = (f32[6,128,256]{2,1,0:T(8,128)S(1)}, f32[6,128,256]{2,1,0:T(8,128)}, u32[]{:S(2)}) copy-start(f32[6,128,256]{2,1,0:T(8,128)} %param.12) | copy-start | bytes 2359300
  10.1 118.4 %all-reduce.16.cloned.1.call-start = ((), (), s32[]{:S(2)}) async-start(), calls=%async_computation.1 | async-start | bytes 1048576 | tf_op jit(solution)/shard_map/psum | solution.py:38
  95.5 0.7 slice-start
  95.5 113.7 %all-reduce.18.cloned.1.call-start = ((), (), s32[]{:S(2)}) async-start(), calls=%async_computation.2 | async-start | bytes 1048576 | tf_op jit(solution)/shard_map/psum | solution.py:28
  136.7 0.7 copy-start.3
  136.7 106.8 %all-reduce.20.cloned.1.call-start = ((), (), s32[]{:S(2)}) async-start(), calls=%async_computation.3 | async-start | bytes 524288 | tf_op jit(solution)/shard_map/psum | solution.py:38
  212.1 106.7 %all-reduce.22.cloned.1.call-start = ((), (), s32[]{:S(2)}) async-start(), calls=%async_computation.4 | async-start | bytes 524288 | tf_op jit(solution)/shard_map/psum | solution.py:28
  248.0 134.7 %all-reduce.24.cloned.1.call-start = ((), (), s32[]{:S(2)}) async-start(), calls=%async_computation.5 | async-start | bytes 262144 | tf_op jit(solution)/shard_map/psum | solution.py:64
  351.9 108.9 %all-reduce.30.cloned.1.call-start = ((), (), s32[]{:S(2)}) async-start(), calls=%async_computation.9 | async-start | bytes 1048576
  388.3 138.7 %all-reduce.26.cloned.1.call-start = ((), (), s32[]{:S(2)}) async-start(), calls=%async_computation.6 | async-start | bytes 524288 | tf_op jit(solution)/shard_map/psum | solution.py:64
  388.4 0.7 copy-start.4
  495.7 115.9 %all-reduce.32.cloned.1.call-start = ((), (), s32[]{:S(2)}) async-start(), calls=%async_computation.10 | async-start | bytes 2097152
  533.2 120.9 %copy-start.1 = (f32[7,128,256]{2,1,0:T(8,128)S(1)}, f32[7,128,256]{2,1,0:T(8,128)}, u32[]{:S(2)}) copy-start(f32[7,128,256]{2,1,0:T(8,128)} %param.11) | copy-start | bytes 2752516
  533.3 120.9 %all-gather.2.cloned.1.call-start = ((), (), s32[]{:S(2)}) async-start(), calls=%async_computation.7 | async-start | bytes 1179648 | tf_op jit(solution)/shard_map/all_gather | solution.py:61
  614.2 75.1 %all-reduce.28.cloned.1.call-start = ((), (), s32[]{:S(2)}) async-start(), calls=%async_computation.8 | async-start | bytes 1048576 | tf_op jit(solution)/shard_map/psum | solution.py:64
Sparse Core Ops, SparseCore 0:
  10.9 80.7 all-reduce.13
  95.6 32.7 all-reduce.15
  136.8 72.3 all-reduce.17
  212.2 31.2 all-reduce.19
  248.2 70.5 all-reduce.21
  352.0 30.6 all-reduce.23
  388.4 72.3 all-reduce.29
  495.8 31.1 all-reduce.25
  533.4 78.1 all-reduce.31
  614.4 39.7 all-gather.1
  657.4 31.8 all-reduce.27
where the time goes:
time: 699 us; the launch traced here: 698 us
  waiting for transfers between devices  571 us (82%)
  blocking collectives  62.6 us (9%)
  local copies, waits for them, and re-layouts  21.2 us (3%)
  matrix products  18.7 us (3%)
  between operations  14.1 us (2%)
  other arithmetic  10.6 us (2%)
    psum x3, waiting for transfers between devices, local(): complete = lax.psum(partial_value, 'leaf')  224 us
    unnamed x13, waiting for transfers between devices  149 us
    psum x3, waiting for transfers between devices, local(): solved = lax.psum(partial_value, 'row')  94.1 us
    psum x2, waiting for transfers between devices, local(): update = lax.psum(update, 'row')  63.6 us
    all_gather x2, blocking collectives, local(): lax.all_gather(residual, 'leaf', axis=0, tiled=True)  62.6 us
    all_gather x1, waiting for transfers between devices, local(): lax.all_gather(residual, 'leaf', axis=0, tiled=True)  39.8 us
  transfers between devices with their start and end apart: 11, of which 11 were waited for; matrix products, arithmetic and copies ran while one was open for 0% of the time, Pallas kernels for 0%

commit v1 on v0

--- a/solution.py
+++ b/solution.py
@@ -2,6 +2,22 @@
 import jax.numpy as jnp
 from jax import lax
 from jax.sharding import PartitionSpec as P
+
+
+def mix_panels(frame_in):
+    block_last, inter = (jax.lax.axis_size("leaf"), jax.lax.axis_index("leaf"))
+    block_out, val = (frame_in, 1)
+    while val < block_last:
+        kept_arr = jax.lax.ppermute(
+            block_out,
+            axis_name="leaf",
+            perm=list(map(lambda dev_j: (dev_j, dev_j ^ val), range(block_last))),
+        )
+        reached = jnp.concatenate([block_out, kept_arr], axis=0)
+        o_now = jnp.concatenate([kept_arr, block_out], axis=0)
+        block_out = jnp.where(inter & val == 0, reached, o_now)
+        val = 2 * val
+    return block_out
 
 
 def local(rhs_blocks, diag_inverse, lower_blocks, update_rows):
@@ -56,10 +72,7 @@
                 tiled=True,
             )
         partial_value = jnp.einsum(
-            "scr,rst->sct",
-            diag_part,
-            lax.all_gather(residual, "leaf", axis=0, tiled=True),
-            precision=lax.Precision.HIGHEST,
+            "scr,rst->sct", diag_part, mix_panels(residual), precision=lax.Precision.HIGHEST
         )
         solved = lax.psum(partial_value, "row")
         answer = answer.at[first_node * panel_rows : stop_node * panel_rows].set(

time: 699 us -> 683 us (0.977)
  blocking collectives: 62.6 us -> 0 us
  waiting for transfers between devices: 571 us -> 611 us
  starting transfers between devices: 0.42 us -> 12.6 us
    ppermute x0 -> x9, waiting for transfers between devices: none -> 78 us  [mix_panels(): jax.lax.ppermute(block_out, axis_name='leaf', perm=list(map(lambda dev_j:...]
    all_gather x2 -> x0, blocking collectives: 62.6 us -> none  [local(): lax.all_gather(residual, 'leaf', axis=0, tiled=True)]
    all_gather x1 -> x0, waiting for transfers between devices: 39.8 us -> none  [local(): lax.all_gather(residual, 'leaf', axis=0, tiled=True)]
    ppermute x0 -> x9, starting transfers between devices: none -> 12.1 us  [mix_panels(): jax.lax.ppermute(block_out, axis_name='leaf', perm=list(map(lambda dev_j:...]
    unnamed x13 -> x12, waiting for transfers between devices: 149 us -> 149 us
  transfers between devices with their start and end apart: 11 -> 19, of which waited for: 11 -> 19; matrix products, arithmetic and copies ran while one was open for 0% -> 0% of each run, Pallas kernels for 0% -> 0%
where the time goes in v1:
time: 683 us
  waiting for transfers between devices  611 us (89%)
  local copies, waits for them, and re-layouts  19.1 us (3%)
  matrix products  15.6 us (2%)
  between operations  14.5 us (2%)
  starting transfers between devices  12.6 us (2%)
  other arithmetic  10 us (1%)
    psum x3, waiting for transfers between devices, local(): complete = lax.psum(partial_value, 'leaf')  224 us
    unnamed x12, waiting for transfers between devices  149 us
    psum x3, waiting for transfers between devices, local(): solved = lax.psum(partial_value, 'row')  96.3 us
    ppermute x9, waiting for transfers between devices, mix_panels(): jax.lax.ppermute(block_out, axis_name='leaf', perm=list(map(lambda dev_j:...  78 us
    psum x2, waiting for transfers between devices, local(): update = lax.psum(update, 'row')  63.6 us
  transfers between devices with their start and end apart: 19, of which 19 were waited for; matrix products, arithmetic and copies ran while one was open for 0% of the time, Pallas kernels for 0%

profile of v1, /device:TPU:0, one launch (start us, length us, event | category | flops | bytes accessed | tf_op | source)
XLA Modules:
  0.0 682.6 jit_solution(10572973923042864874)
XLA Ops:
  6.5 1.3 copy.68
  8.0 2.0 convolution_bitcast_fusion.1
  10.1 81.5 %all-reduce.14.cloned.1.call-done = f32[256,4,256]{0,2,1:T(8,128)} async-done(((f32[256,4,256]{0,2,1:T(8,128)}), f32[256,4,256]{0,2,1:T(8,128)}) %all-reduce.14.cloned.1.call-update) | async-done | bytes 1048592 | tf_op jit(solution)/shard_map/psum | solution.py:44
  91.6 3.1 convolution_bitcast_fusion.4
  94.8 0.6 slice-done
  95.4 32.2 %all-reduce.16.cloned.1.call-done = f32[4,128,256]{1,2,0:T(8,128)} async-done(((f32[4,128,256]{1,2,0:T(8,128)}), f32[4,128,256]{1,2,0:T(8,128)}) %all-reduce.16.cloned.1.call-update) | async-done | bytes 524304 | tf_op jit(solution)/shard_map/psum | solution.py:54
  127.7 1.1 neg.12
  128.9 3.7 scatter_fusion
  132.7 1.4 convolution_bitcast_fusion.3
  134.2 0.6 copy-done.7
  134.8 71.9 %all-reduce.18.cloned.1.call-done = f32[256,2,256]{0,2,1:T(8,128)} async-done(((f32[256,2,256]{0,2,1:T(8,128)}), f32[256,2,256]{0,2,1:T(8,128)}) %all-reduce.18.cloned.1.call-update) | async-done | bytes 524304 | tf_op jit(solution)/shard_map/psum | solution.py:44
  206.7 2.3 convolution_bitcast_fusion.5
  209.1 31.3 %all-reduce.20.cloned.1.call-done = f32[2,128,256]{1,2,0:T(8,128)} async-done(((f32[2,128,256]{1,2,0:T(8,128)}), f32[2,128,256]{1,2,0:T(8,128)}) %all-reduce.20.cloned.1.call-update) | async-done | bytes 262160 | tf_op jit(solution)/shard_map/psum | solution.py:54
  240.4 1.0 neg.14
  241.5 2.3 scatter_fusion.1
  243.9 1.1 convolution_bitcast_fusion.6
  245.1 70.6 %all-reduce.22.cloned.1.call-done = f32[256,1,256]{0,2,1:T(8,128)} async-done(((f32[256,1,256]{0,2,1:T(8,128)}), f32[256,1,256]{0,2,1:T(8,128)}) %all-reduce.22.cloned.1.call-update) | async-done | bytes 262160 | tf_op jit(solution)/shard_map/psum | solution.py:44
  315.7 1.1 constant_dynamic-slice_fusion
  316.8 0.8 collective-permute-start
  317.7 4.1 collective-permute-done
  322.0 1.1 collective-permute-start.1
  323.2 4.4 collective-permute-done.1
  327.7 2.4 collective-permute-start.2
  330.3 4.8 collective-permute-done.2
  335.1 1.0 convolution_bitcast_fusion.7
  336.2 31.5 %all-reduce.24.cloned.1.call-done = f32[128,256]{0,1:T(8,128)} async-done(((f32[128,256]{0,1:T(8,128)}), f32[128,256]{0,1:T(8,128)}) %all-reduce.24.cloned.1.call-update) | async-done | bytes 131088 | tf_op jit(solution)/shard_map/psum | solution.py:77
  367.7 1.0 scatter.10
  368.7 0.3 copy.32
  369.0 1.0 gather_fusion
  370.0 0.6 convolution_bitcast_fusion.2
  370.6 1.0 copy.34
  371.9 0.6 copy-done.8
  372.5 0.6 dynamic-slice.20
  373.7 70.4 %all-reduce.30.cloned.1.call-done = f32[256,2,256]{2,1,0:T(2,128)} async-done(((f32[256,2,256]{2,1,0:T(2,128)}), f32[256,2,256]{2,1,0:T(2,128)}) %all-reduce.30.cloned.1.call-update) | async-done | bytes 524304
  444.2 0.8 constant_dynamic-slice_fusion.2
  445.3 1.0 collective-permute-start.3
  446.3 5.5 collective-permute-done.3
  452.0 1.0 collective-permute-start.4
  453.0 6.5 collective-permute-done.4
  459.7 1.6 collective-permute-start.5
  461.3 8.6 %collective-permute-done.5 = f32[128,2,256]{0,2,1:T(8,128)S(1)} collective-permute-done((f32[128,2,256]{0,2,1:T(8,128)S(1)}, f32[128,2,256]{0,2,1:T(8,128)S(1)}, u32[]{:S(2)}, u32[]{:S(2)}) %collective-permute-start.5) | collective-permute-done | bytes 262176 | tf_op jit(solution)/shard_map/ppermute | solution.py:11
  469.8 1.7 fusion.6
  471.5 0.8 copy.50
  472.4 31.5 %all-reduce.26.cloned.1.call-done = f32[256,256]{0,1:T(8,128)} async-done(((f32[256,256]{0,1:T(8,128)}), f32[256,256]{0,1:T(8,128)}) %all-reduce.26.cloned.1.call-update) | async-done | bytes 262160 | tf_op jit(solution)/shard_map/psum | solution.py:77
  503.9 1.0 constant_dynamic-update-slice_fusion.1
  504.9 0.3 copy.38
  505.2 1.6 gather_fusion.1
  506.8 1.0 convolution_bitcast_fusion
  507.8 1.3 copy.40
  509.2 78.2 %all-reduce.32.cloned.1.call-done = f32[256,4,256]{2,1,0:T(4,128)} async-done(((f32[256,4,256]{2,1,0:T(4,128)}), f32[256,4,256]{2,1,0:T(4,128)}) %all-reduce.32.cloned.1.call-update) | async-done | bytes 1048592
  587.4 0.9 constant_dynamic-slice_fusion.1
  588.8 1.3 collective-permute-start.6
  590.1 11.7 %collective-permute-done.6 = f32[32,4,256]{0,2,1:T(8,128)S(1)} collective-permute-done((f32[32,4,256]{0,2,1:T(8,128)S(1)}, f32[32,4,256]{0,2,1:T(8,128)S(1)}, u32[]{:S(2)}, u32[]{:S(2)}) %collective-permute-start.6) | collective-permute-done | bytes 131104 | tf_op jit(solution)/shard_map/ppermute | solution.py:11
  601.8 0.3 maximum_select_fusion.4
  602.2 0.7 collective-permute-start.7
  602.9 11.4 %collective-permute-done.7 = f32[64,4,256]{0,2,1:T(8,128)S(1)} collective-permute-done((f32[64,4,256]{0,2,1:T(8,128)S(1)}, f32[64,4,256]{0,2,1:T(8,128)S(1)}, u32[]{:S(2)}, u32[]{:S(2)}) %collective-permute-start.7) | collective-permute-done | bytes 262176 | tf_op jit(solution)/shard_map/ppermute | solution.py:11
  614.3 0.3 maximum_select_fusion.5
  614.6 2.1 collective-permute-start.8
  616.7 21.1 %collective-permute-done.8 = f32[128,4,256]{0,2,1:T(8,128)S(1)} collective-permute-done((f32[128,4,256]{0,2,1:T(8,128)S(1)}, f32[128,4,256]{0,2,1:T(8,128)S(1)}, u32[]{:S(2)}, u32[]{:S(2)}) %collective-permute-start.8) | collective-permute-done | bytes 524320 | tf_op jit(solution)/shard_map/ppermute | solution.py:11
  637.8 1.3 fusion
  639.1 1.0 copy.51
  640.1 33.3 %all-reduce.28.cloned.1.call-done = f32[512,256]{0,1:T(8,128)} async-done(((f32[512,256]{0,1:T(8,128)}), f32[512,256]{0,1:T(8,128)}) %all-reduce.28.cloned.1.call-update) | async-done | bytes 524304 | tf_op jit(solution)/shard_map/psum | solution.py:77
  673.4 1.1 constant_dynamic-update-slice_fusion
  674.5 1.2 copy.44
  (56 shorter events, 3.0 us)
Async XLA Ops:
  6.5 1.5 copy-start.3
  6.5 85.1 %all-reduce.14.cloned.1.call-start = ((), (), s32[]{:S(2)}) async-start(), calls=%async_computation | async-start | bytes 2097152 | tf_op jit(solution)/shard_map/psum | solution.py:44
  10.0 81.6 %copy-start = (f32[6,128,256]{2,1,0:T(8,128)S(1)}, f32[6,128,256]{2,1,0:T(8,128)}, u32[]{:S(2)}) copy-start(f32[6,128,256]{2,1,0:T(8,128)} %param.12) | copy-start | bytes 2359300
  10.0 117.6 %all-reduce.16.cloned.1.call-start = ((), (), s32[]{:S(2)}) async-start(), calls=%async_computation.1 | async-start | bytes 1048576 | tf_op jit(solution)/shard_map/psum | solution.py:54
  94.7 0.7 slice-start
  94.7 111.9 %all-reduce.18.cloned.1.call-start = ((), (), s32[]{:S(2)}) async-start(), calls=%async_computation.2 | async-start | bytes 1048576 | tf_op jit(solution)/shard_map/psum | solution.py:44
  128.9 3.7 copy-start.4
  134.1 0.7 copy-start.7
  134.1 106.3 %all-reduce.20.cloned.1.call-start = ((), (), s32[]{:S(2)}) async-start(), calls=%async_computation.3 | async-start | bytes 524288 | tf_op jit(solution)/shard_map/psum | solution.py:54
  209.0 106.7 %all-reduce.22.cloned.1.call-start = ((), (), s32[]{:S(2)}) async-start(), calls=%async_computation.4 | async-start | bytes 524288 | tf_op jit(solution)/shard_map/psum | solution.py:44
  245.0 122.7 %all-reduce.24.cloned.1.call-start = ((), (), s32[]{:S(2)}) async-start(), calls=%async_computation.5 | async-start | bytes 262144 | tf_op jit(solution)/shard_map/psum | solution.py:77
  315.7 1.9 copy-start.6
  316.8 5.0 collective-permute-start
  322.0 5.6 collective-permute-start.1
  327.7 7.3 %collective-permute-start.2 = (f32[128,1,256]{0,2,1:T(8,128)S(1)}, f32[128,1,256]{0,2,1:T(8,128)S(1)}, u32[]{:S(2)}, u32[]{:S(2)}) collective-permute-start(f32[128,1,256]{0,2,1:T(8,128)S(1)} %maximum_select_fusion.13), channel_id=1, source_target_pairs={{0,16},{4,20},{8,24},{12,28},{16,0},{20,4},{24,8},{28,12},{1,17},{... | collective-permute-start | bytes 393224 | tf_op jit(solution)/shard_map/ppermute | solution.py:11
  336.1 108.0 %all-reduce.30.cloned.1.call-start = ((), (), s32[]{:S(2)}) async-start(), calls=%async_computation.8 | async-start | bytes 1048576
  371.6 73.6 %copy-start.2 = (f32[256,2,256]{0,2,1:T(8,128)S(1)}, f32[256,2,256]{0,2,1:T(8,128)}, u32[]{:S(2)}) copy-start(f32[256,2,256]{0,2,1:T(8,128)} %all-reduce.18.cloned.1.call-done) | copy-start | bytes 1572868
  371.6 132.3 %all-reduce.26.cloned.1.call-start = ((), (), s32[]{:S(2)}) async-start(), calls=%async_computation.6 | async-start | bytes 524288 | tf_op jit(solution)/shard_map/psum | solution.py:77
  371.9 0.7 copy-start.8
  445.3 6.4 collective-permute-start.3
  452.0 7.5 %collective-permute-start.4 = (f32[64,2,256]{0,2,1:T(8,128)S(1)}, f32[64,2,256]{0,2,1:T(8,128)S(1)}, u32[]{:S(2)}, u32[]{:S(2)}) collective-permute-start(f32[64,2,256]{0,2,1:T(8,128)S(1)} %maximum_select_fusion.8), channel_id=1, source_target_pairs={{0,8},{4,12},{8,0},{12,4},{16,24},{20,28},{24,16},{28,20},{1,9},{5... | collective-permute-start | bytes 393224 | tf_op jit(solution)/shard_map/ppermute | solution.py:11
  459.7 10.1 %collective-permute-start.5 = (f32[128,2,256]{0,2,1:T(8,128)S(1)}, f32[128,2,256]{0,2,1:T(8,128)S(1)}, u32[]{:S(2)}, u32[]{:S(2)}) collective-permute-start(f32[128,2,256]{0,2,1:T(8,128)S(1)} %maximum_select_fusion.9), channel_id=1, source_target_pairs={{0,16},{4,20},{8,24},{12,28},{16,0},{20,4},{24,8},{28,12},{1,17},{... | collective-permute-start | bytes 786440 | tf_op jit(solution)/shard_map/ppermute | solution.py:11
  472.4 115.1 %all-reduce.32.cloned.1.call-start = ((), (), s32[]{:S(2)}) async-start(), calls=%async_computation.9 | async-start | bytes 2097152
  509.1 79.4 %copy-start.1 = (f32[256,4,256]{0,2,1:T(8,128)S(1)}, f32[256,4,256]{0,2,1:T(8,128)}, u32[]{:S(2)}) copy-start(f32[256,4,256]{0,2,1:T(8,128)} %all-reduce.14.cloned.1.call-done) | copy-start | bytes 3145732
  509.1 164.3 %all-reduce.28.cloned.1.call-start = ((), (), s32[]{:S(2)}) async-start(), calls=%async_computation.7 | async-start | bytes 1048576 | tf_op jit(solution)/shard_map/psum | solution.py:77
  588.8 13.0 %collective-permute-start.6 = (f32[32,4,256]{0,2,1:T(8,128)S(1)}, f32[32,4,256]{0,2,1:T(8,128)S(1)}, u32[]{:S(2)}, u32[]{:S(2)}) collective-permute-start(f32[32,4,256]{0,2,1:T(8,128)S(1)} %dynamic-slice_subtract_fusion), channel_id=1, source_target_pairs={{0,4},{4,0},{8,12},{12,8},{16,20},{20,16},{24,28},{28,24},{1,5},{5... | collective-permute-start | bytes 393224 | tf_op jit(solution)/shard_map/ppermute | solution.py:11
  602.2 35.7 %copy-start.5 = (f32[7,128,256]{2,1,0:T(8,128)S(1)}, f32[7,128,256]{2,1,0:T(8,128)}, u32[]{:S(2)}) copy-start(f32[7,128,256]{2,1,0:T(8,128)} %param.11) | copy-start | bytes 2752516
  602.2 12.1 %collective-permute-start.7 = (f32[64,4,256]{0,2,1:T(8,128)S(1)}, f32[64,4,256]{0,2,1:T(8,128)S(1)}, u32[]{:S(2)}, u32[]{:S(2)}) collective-permute-start(f32[64,4,256]{0,2,1:T(8,128)S(1)} %maximum_select_fusion.4), channel_id=1, source_target_pairs={{0,8},{4,12},{8,0},{12,4},{16,24},{20,28},{24,16},{28,20},{1,9},{5... | collective-permute-start | bytes 786440 | tf_op jit(solution)/shard_map/ppermute | solution.py:11
  614.6 23.2 %collective-permute-start.8 = (f32[128,4,256]{0,2,1:T(8,128)S(1)}, f32[128,4,256]{0,2,1:T(8,128)S(1)}, u32[]{:S(2)}, u32[]{:S(2)}) collective-permute-start(f32[128,4,256]{0,2,1:T(8,128)S(1)} %maximum_select_fusion.5), channel_id=1, source_target_pairs={{0,16},{4,20},{8,24},{12,28},{16,0},{20,4},{24,8},{28,12},{1,17},{... | collective-permute-start | bytes 1572872 | tf_op jit(solution)/shard_map/ppermute | solution.py:11
Sparse Core Ops, SparseCore 0:
  10.9 80.7 all-reduce.13
  94.8 32.7 all-reduce.15
  134.2 72.3 all-reduce.17
  209.2 31.2 all-reduce.19
  245.1 70.5 all-reduce.21
  336.2 31.4 all-reduce.23
  371.8 72.3 all-reduce.29
  472.5 31.3 all-reduce.25
  509.3 78.1 all-reduce.31
  640.3 33.1 all-reduce.27
